TPU v7x, 256 devices: a whole 4x4x8 slice. The times are simulated.
256 devices in a mesh: dp: 32 (over z_hi, x, core), seq: 8 (over y, z_lo).
Axes of the slice: x: 4, y: 4, z: 8 (z_hi: 4, z_lo: 2; z = z_hi * 2 + z_lo), core: 2. Of those that a mesh axis runs over, the one named last changes fastest.
Arguments:
- q_proj: bfloat16 [32, 1024, 4096], P('dp', 'seq'), may hold values from -200 to 200
- k_proj: bfloat16 [32, 1024, 512], P('dp', 'seq'), may hold values from -6 to 6
- v_proj: bfloat16 [32, 1024, 512], P('dp', 'seq'), may hold values from -6 to 6
- cache_k: bfloat16 [32, 1024, 512], P('dp', 'seq'), may hold values from -6 to 6
- cache_v: bfloat16 [32, 1024, 512], P('dp', 'seq'), may hold values from -6 to 6
- bias_q: bfloat16 [4096], replicated, may hold values from -3 to 3
- bias_k: bfloat16 [512], replicated, may hold values from -3 to 3
- bias_v: bfloat16 [512], replicated, may hold values from -3 to 3
- start: int32 [32], P('dp'), may hold values from 256 to 1024, as said below
- dout: bfloat16 [32, 1024, 4096], P('dp', 'seq'), may hold values from -6 to 6
Outputs:
- attn_out: bfloat16 [32, 1024, 4096], P('dp', 'seq')
- grad_q: bfloat16 [32, 1024, 4096], P('dp', 'seq')
- grad_k: bfloat16 [32, 1024, 512], P('dp', 'seq')
- grad_v: bfloat16 [32, 1024, 512], P('dp', 'seq')
- grad_bias_q: float32 [4096], replicated
- grad_bias_k: float32 [512], replicated
- grad_bias_v: float32 [512], replicated
Inputs may be any that keep to these rules, and one draw needn't show every extreme that they name: Cache slots at and beyond start hold no prefix; some sequence has a full prefix of 1024 slots.
All inputs are finite; a program needn't handle non-finite values.
Results may differ from a plain program's by a relative error of at most 0.04.
The roundings to bfloat16 on the way count: a program that leaves them out, or rounds other values in their place, can miss the bound.
Values may be sent and summed in bfloat16 or wider, within the bound.
A program may use at most 128 MiB of HBM per device.

v0:
```python
import jax
import jax.numpy as jnp
from jax import lax
from jax.sharding import PartitionSpec as P

HQ = 32
KV = 4
HD = 128
GROUP = 8


def rotary_tables(positions, width):
    half = width // 2
    freqs = jnp.exp(
        -(2.0 * jnp.arange(half, dtype=jnp.float32) / width) * jnp.log(jnp.float32(1000000.0))
    )
    angles = positions.astype(jnp.float32)[:, None] * freqs[None, :]
    cosine = jnp.concatenate([jnp.cos(angles), jnp.cos(angles)], axis=1)
    sine = jnp.concatenate([jnp.sin(angles), jnp.sin(angles)], axis=1)
    return (cosine[:, None, :], sine[:, None, :])


def rotary(values, positions):
    cosine, sine = rotary_tables(positions, values.shape[2])
    half = values.shape[2] // 2
    turned = jnp.concatenate([-values[:, :, half:], values[:, :, :half]], axis=2)
    return values * cosine + turned * sine


def rotary_back(grads, positions):
    cosine, sine = rotary_tables(positions, grads.shape[2])
    half = grads.shape[2] // 2
    scaled = grads * sine
    turned = jnp.concatenate([scaled[:, :, half:], -scaled[:, :, :half]], axis=2)
    return grads * cosine + turned


def attend(queries, cotangent, keys, values, first, row_zero, prefix):
    rows, heads, width = queries.shape
    key_count = keys.shape[0]
    slab = key_count - prefix
    head_block = max(1, min(512 // rows, GROUP, heads))
    row_block = min(rows, 512)
    scale = width ** (-0.5)
    key_index = jnp.arange(key_count, dtype=jnp.int32)

    def head_step(carry, head_slot):
        key_acc, value_acc = carry
        head_zero = head_slot * head_block
        owner = head_zero // GROUP
        key_one = lax.dynamic_index_in_dim(keys, owner, 1, keepdims=False)
        value_one = lax.dynamic_index_in_dim(values, owner, 1, keepdims=False)
        query_part = lax.dynamic_slice_in_dim(queries, head_zero, head_block, 1)
        cot_part = lax.dynamic_slice_in_dim(cotangent, head_zero, head_block, 1)

        def row_step(inner, row_slot):
            grad_key, grad_value = inner
            offset = row_slot * row_block
            query_rows = lax.dynamic_slice_in_dim(query_part, offset, row_block, 0)
            cot_rows = lax.dynamic_slice_in_dim(cot_part, offset, row_block, 0)
            query_index = row_zero + offset + jnp.arange(row_block, dtype=jnp.int32)
            allowed = jnp.where(
                key_index[None, :] < prefix,
                key_index[None, :] < first,
                key_index[None, :] - prefix <= query_index[:, None],
            )
            scores = (
                jnp.einsum("rhd,kd->hrk", query_rows, key_one, preferred_element_type=jnp.float32)
                * scale
            )
            scores = jnp.where(allowed[None], scores, -1e30)
            highest = jnp.max(scores, axis=-1, keepdims=True)
            expo = jnp.exp(scores - highest)
            probs = expo / jnp.sum(expo, axis=-1, keepdims=True)
            probs_b = probs.astype(jnp.bfloat16)
            output = jnp.einsum(
                "hrk,kd->rhd", probs_b, value_one, preferred_element_type=jnp.float32
            ).astype(jnp.bfloat16)
            delta = jnp.sum(cot_rows.astype(jnp.float32) * output.astype(jnp.float32), axis=-1).T
            dprobs = jnp.einsum(
                "rhd,kd->hrk", cot_rows, value_one, preferred_element_type=jnp.float32
            )
            dscore = (probs * (dprobs - delta[:, :, None])).astype(jnp.bfloat16)
            grad_query = (
                jnp.einsum("hrk,kd->rhd", dscore, key_one, preferred_element_type=jnp.float32)
                * scale
            ).astype(jnp.bfloat16)
            grad_key = (
                grad_key
                + jnp.einsum(
                    "hrk,rhd->kd",
                    dscore[:, :, prefix:],
                    query_rows,
                    preferred_element_type=jnp.float32,
                )
                * scale
            )
            grad_value = grad_value + jnp.einsum(
                "hrk,rhd->kd", probs_b[:, :, prefix:], cot_rows, preferred_element_type=jnp.float32
            )
            return ((grad_key, grad_value), (output, grad_query))

        empty = jnp.zeros((slab, width), jnp.float32)
        (grad_key, grad_value), (outputs, grads) = lax.scan(
            row_step, (empty, empty), jnp.arange(rows // row_block, dtype=jnp.int32)
        )
        outputs = outputs.reshape(rows, head_block, width)
        grads = grads.reshape(rows, head_block, width)
        old_key = lax.dynamic_index_in_dim(key_acc, owner, 1, keepdims=False)
        old_value = lax.dynamic_index_in_dim(value_acc, owner, 1, keepdims=False)
        key_acc = lax.dynamic_update_index_in_dim(key_acc, old_key + grad_key, owner, 1)
        value_acc = lax.dynamic_update_index_in_dim(value_acc, old_value + grad_value, owner, 1)
        return ((key_acc, value_acc), (outputs, grads))

    zeros_kv = jnp.zeros((slab, keys.shape[1], width), jnp.float32)
    (key_acc, value_acc), (outputs, grads) = lax.scan(
        head_step, (zeros_kv, zeros_kv), jnp.arange(heads // head_block, dtype=jnp.int32)
    )
    outputs = jnp.transpose(outputs, (1, 0, 2, 3)).reshape(rows, heads, width)
    grads = jnp.transpose(grads, (1, 0, 2, 3)).reshape(rows, heads, width)
    return (outputs, grads, key_acc, value_acc)


def body(q_proj, k_proj, v_proj, cache_k, cache_v, bias_q, bias_k, bias_v, start, dout):
    devices = lax.axis_size("seq")
    rank = lax.axis_index("seq")
    tokens = q_proj.shape[1]
    first = start[0]
    positions = first + rank * tokens + jnp.arange(tokens, dtype=jnp.int32)
    queries = rotary(
        (q_proj[0].astype(jnp.float32) + bias_q.astype(jnp.float32)).reshape(tokens, HQ, HD),
        positions,
    ).astype(jnp.bfloat16)
    keys = rotary(
        (k_proj[0].astype(jnp.float32) + bias_k.astype(jnp.float32)).reshape(tokens, KV, HD),
        positions,
    ).astype(jnp.bfloat16)
    values = (
        (v_proj[0].astype(jnp.float32) + bias_v.astype(jnp.float32))
        .astype(jnp.bfloat16)
        .reshape(tokens, KV, HD)
    )
    cotangent = dout[0].reshape(tokens, HQ, HD)
    cached_keys = cache_k[0].reshape(cache_k.shape[1], KV, HD)
    cached_values = cache_v[0].reshape(cache_v.shape[1], KV, HD)
    copies = max(devices // KV, 1)
    keys_wide = jnp.repeat(keys, copies, axis=1)
    values_wide = jnp.repeat(values, copies, axis=1)
    cache_keys_wide = jnp.repeat(cached_keys, copies, axis=1)
    cache_values_wide = jnp.repeat(cached_values, copies, axis=1)
    head_queries, head_keys, head_values, head_cot = (
        lax.all_to_all(queries, "seq", split_axis=1, concat_axis=0, tiled=True),
        lax.all_to_all(keys_wide, "seq", split_axis=1, concat_axis=0, tiled=True),
        lax.all_to_all(values_wide, "seq", split_axis=1, concat_axis=0, tiled=True),
        lax.all_to_all(cotangent, "seq", split_axis=1, concat_axis=0, tiled=True),
    )
    head_cache_keys, head_cache_values = (
        lax.all_to_all(cache_keys_wide, "seq", split_axis=1, concat_axis=0, tiled=True),
        lax.all_to_all(cache_values_wide, "seq", split_axis=1, concat_axis=0, tiled=True),
    )
    prefix = head_cache_keys.shape[0]
    all_keys = jnp.concatenate([head_cache_keys, head_keys], axis=0)
    all_values = jnp.concatenate([head_cache_values, head_values], axis=0)
    outputs, dq_rot, dk_rot, dv_all = attend(
        head_queries, head_cot, all_keys, all_values, first, 0, prefix
    )
    out_tokens, dq_tokens = (
        lax.all_to_all(outputs, "seq", split_axis=0, concat_axis=1, tiled=True),
        lax.all_to_all(dq_rot, "seq", split_axis=0, concat_axis=1, tiled=True),
    )
    dk_copies, dv_copies = (
        lax.all_to_all(
            dk_rot.astype(jnp.bfloat16), "seq", split_axis=0, concat_axis=1, tiled=True
        ).astype(dk_rot.dtype),
        lax.all_to_all(
            dv_all.astype(jnp.bfloat16), "seq", split_axis=0, concat_axis=1, tiled=True
        ).astype(dv_all.dtype),
    )
    dk_tokens = jnp.sum(dk_copies.reshape(tokens, KV, copies, HD), axis=2)
    dv_tokens = jnp.sum(dv_copies.reshape(tokens, KV, copies, HD), axis=2)
    grad_query = rotary_back(dq_tokens.astype(jnp.float32), positions)
    grad_key = rotary_back(dk_tokens, positions)
    sums_query, sums_key, sums_value = lax.psum(
        (
            jnp.sum(grad_query, axis=0).reshape(HQ * HD),
            jnp.sum(grad_key, axis=0).reshape(KV * HD),
            jnp.sum(dv_tokens, axis=0).reshape(KV * HD),
        ),
        ("dp", "seq"),
    )
    return (
        out_tokens.reshape(1, tokens, HQ * HD),
        grad_query.astype(jnp.bfloat16).reshape(1, tokens, HQ * HD),
        grad_key.astype(jnp.bfloat16).reshape(1, tokens, KV * HD),
        dv_tokens.astype(jnp.bfloat16).reshape(1, tokens, KV * HD),
        sums_query,
        sums_key,
        sums_value,
    )


def solution(mesh):
    placed = (
        P("dp", "seq", None),
        P("dp", "seq", None),
        P("dp", "seq", None),
        P("dp", "seq", None),
        P("dp", "seq", None),
        P(),
        P(),
        P(),
        P("dp"),
        P("dp", "seq", None),
    )
    return jax.shard_map(
        body,
        mesh=mesh,
        in_specs=placed,
        out_specs=(
            P("dp", "seq", None),
            P("dp", "seq", None),
            P("dp", "seq", None),
            P("dp", "seq", None),
            P(),
            P(),
            P(),
        ),
        check_vma=False,
    )
```

profile of v0, /device:TPU:1, one launch (start us, length us, event | category | flops | bytes accessed | tf_op | source)
XLA Modules:
  0.0 376.5 jit_solution(17324488417311112449)
XLA Ops:
  2.4 6.5 %all-to-all-start.2 = ((bf16[128,8,128]{2,0,1:T(8,128)(2,1)}), bf16[128,8,128]{2,0,1:T(8,128)(2,1)S(1)}, u32[]{:S(2)}, u32[]{:S(2)}) async-start(bf16[128,8,128]{2,0,1:T(8,128)(2,1)} %bitcast.11), calls=%async_computation.2 | async-start | bytes 524288 | tf_op jit(solution)/shard_map/all_to_all | solution.py:158
  15.8 3.4 all-to-all-start.4
  19.3 6.0 %all-to-all-done.4 = bf16[128,8,128]{2,0,1:T(8,128)(2,1)S(1)} async-done(((bf16[128,8,128]{2,0,1:T(8,128)(2,1)}), bf16[128,8,128]{2,0,1:T(8,128)(2,1)S(1)}, u32[]{:S(2)}, u32[]{:S(2)}) %all-to-all-start.4) | async-done | bytes 262176 | tf_op jit(solution)/shard_map/all_to_all | solution.py:159
  26.1 3.4 all-to-all-start.5
  29.8 5.8 %all-to-all-done.5 = bf16[128,8,128]{2,0,1:T(8,128)(2,1)S(1)} async-done(((bf16[128,8,128]{2,0,1:T(8,128)(2,1)}), bf16[128,8,128]{2,0,1:T(8,128)(2,1)S(1)}, u32[]{:S(2)}, u32[]{:S(2)}) %all-to-all-start.5) | async-done | bytes 262176 | tf_op jit(solution)/shard_map/all_to_all | solution.py:154
  36.4 3.4 all-to-all-start.3
  41.2 4.7 %all-to-all-done.3 = bf16[128,8,128]{2,0,1:T(8,128)(2,1)S(1)} async-done(((bf16[128,8,128]{2,0,1:T(8,128)(2,1)}), bf16[128,8,128]{2,0,1:T(8,128)(2,1)S(1)}, u32[]{:S(2)}, u32[]{:S(2)}) %all-to-all-start.3) | async-done | bytes 262176 | tf_op jit(solution)/shard_map/all_to_all | solution.py:153
  45.9 3.7 all-to-all-start.1
  53.5 6.5 %all-to-all-done.1 = bf16[128,32,128]{0,2,1:T(8,128)(2,1)S(1)} async-done(((bf16[128,32,128]{0,2,1:T(8,128)(2,1)}), bf16[128,32,128]{0,2,1:T(8,128)(2,1)S(1)}, u32[]{:S(2)}, u32[]{:S(2)}) %all-to-all-start.1) | async-done | bytes 1048608 | tf_op jit(solution)/shard_map/all_to_all | solution.py:155
  60.0 3.6 all-to-all-start
  66.7 7.2 %all-to-all-done = bf16[128,32,128]{2,0,1:T(8,128)(2,1)S(1)} async-done(((bf16[128,32,128]{2,0,1:T(8,128)(2,1)}), bf16[128,32,128]{2,0,1:T(8,128)(2,1)S(1)}, u32[]{:S(2)}, u32[]{:S(2)}) %all-to-all-start) | async-done | bytes 1048608 | tf_op jit(solution)/shard_map/all_to_all | solution.py:152
  75.0 139.6 %while.59 = (s32[]{:T(128)}, f32[1024,1,128]{2,0,1:T(8,128)S(1)}, f32[1024,1,128]{2,0,1:T(8,128)S(1)}, bf16[4,1024,1,128]{3,1,2,0:T(8,128)(2,1)}, bf16[4,1024,1,...) while((s32[]{:T(128)}, f32[1024,1,128]{2,0,1:T(8,128)S(1)}, ...), condition=%wide.region_6.7_spmd.clone.clone, body=%wide.region_0.6_spmd.clone.clone.sunk | while | flops 1359287296 | bytes 49224388 | solution.py:116
  79.6 28.5 %while.60 = (s32[]{:T(128)}, f32[1024,128]{1,0:T(8,128)S(1)}, f32[1024,128]{1,0:T(8,128)S(1)}, bf16[2,512,1,128]{3,1,0,2:T(8,128)(2,1)}, bf16[2,512,1,128]{3,1,2...) while((s32[]{:T(128)}, f32[1024,128]{1,0:T(8,128)S(1)}, ...), condition=%wide.region_5.5_spmd.clone.clone, body=%wide.region_1.4_spmd.clone.clone.sunk | while | flops 1359025152 | bytes 41875732 | solution.py:104
  90.1 3.1 fusion.81
  104.4 3.1 fusion.81
  114.5 28.5 %while.60 = (s32[]{:T(128)}, f32[1024,128]{1,0:T(8,128)S(1)}, f32[1024,128]{1,0:T(8,128)S(1)}, bf16[2,512,1,128]{3,1,0,2:T(8,128)(2,1)}, bf16[2,512,1,128]{3,1,2...) while((s32[]{:T(128)}, f32[1024,128]{1,0:T(8,128)S(1)}, ...), condition=%wide.region_5.5_spmd.clone.clone, body=%wide.region_1.4_spmd.clone.clone.sunk | while | flops 1359025152 | bytes 41875732 | solution.py:104
  125.0 3.1 fusion.81
  139.3 3.1 fusion.81
  149.4 28.5 %while.60 = (s32[]{:T(128)}, f32[1024,128]{1,0:T(8,128)S(1)}, f32[1024,128]{1,0:T(8,128)S(1)}, bf16[2,512,1,128]{3,1,0,2:T(8,128)(2,1)}, bf16[2,512,1,128]{3,1,2...) while((s32[]{:T(128)}, f32[1024,128]{1,0:T(8,128)S(1)}, ...), condition=%wide.region_5.5_spmd.clone.clone, body=%wide.region_1.4_spmd.clone.clone.sunk | while | flops 1359025152 | bytes 41875732 | solution.py:104
  174.2 3.1 fusion.81
  184.3 28.5 %while.60 = (s32[]{:T(128)}, f32[1024,128]{1,0:T(8,128)S(1)}, f32[1024,128]{1,0:T(8,128)S(1)}, bf16[2,512,1,128]{3,1,0,2:T(8,128)(2,1)}, bf16[2,512,1,128]{3,1,2...) while((s32[]{:T(128)}, f32[1024,128]{1,0:T(8,128)S(1)}, ...), condition=%wide.region_5.5_spmd.clone.clone, body=%wide.region_1.4_spmd.clone.clone.sunk | while | flops 1359025152 | bytes 41875732 | solution.py:104
  209.1 3.1 fusion.81
  216.8 3.4 all-to-all-start.8
  221.8 4.5 %all-to-all-done.8 = bf16[8,2,8192]{2,1,0:T(2,128)(2,1)S(1)} async-done(((bf16[8,2,8192]{2,1,0:T(2,128)(2,1)}), bf16[8,2,8192]{2,1,0:T(2,128)(2,1)S(1)}, u32[]{:S(2)}, u32[]{:S(2)}) %all-to-all-start.8) | async-done | bytes 262176 | tf_op jit(solution)/shard_map/all_to_all | solution.py:172
  226.3 3.6 all-to-all-start.9
  229.9 3.1 copy.153
  233.0 3.2 all-to-all-done.9
  236.2 3.6 all-to-all-start.6
  241.6 9.9 %all-to-all-done.6 = bf16[1024,4,128]{2,1,0:T(4,128)(2,1)S(1)} async-done(((bf16[1024,4,128]{2,1,0:T(4,128)(2,1)}), bf16[1024,4,128]{2,1,0:T(4,128)(2,1)S(1)}, u32[]{:S(2)}, u32[]{:S(2)}) %all-to-all-start.6) | async-done | bytes 1048608 | tf_op jit(solution)/shard_map/all_to_all | solution.py:168
  251.5 3.6 all-to-all-start.7
  273.0 3.2 copy.163
  286.0 90.5 %all-reduce = (f32[4096]{0:T(1024)}, f32[512]{0:T(512)}, f32[512]{0:T(512)}) all-reduce(f32[4096]{0:T(1024)S(1)} %bitcast.274, f32[512]{0:T(512)S(1)} %bitcast.276, f32[512]{0:T(512)S(1)} %bitcast.277), channel_id=1, replica_groups=mesh['dp'=32,'seq'=8] {'dp','seq'}, use_global_device_ids=true, to_apply=%region_10.11 | all-reduce | flops 5120 | bytes 40960 | tf_op jit(solution)/shard_map/psum | solution.py:183
  (322 shorter events, 159.2 us)
Async XLA Ops:
  0.6 10.7 %copy-start.22 = (bf16[1,128,512]{2,1,0:T(8,128)(2,1)S(1)}, bf16[1,128,512]{2,1,0:T(8,128)(2,1)}, u32[]{:S(2)}) copy-start(bf16[1,128,512]{2,1,0:T(8,128)(2,1)} %param.15) | copy-start | bytes 393220
  0.6 10.9 %copy-start.23 = (bf16[1,128,512]{2,1,0:T(8,128)(2,1)S(1)}, bf16[1,128,512]{2,1,0:T(8,128)(2,1)}, u32[]{:S(2)}) copy-start(bf16[1,128,512]{2,1,0:T(8,128)(2,1)} %param.18) | copy-start | bytes 393220
  2.4 16.9 %copy-start.25 = (bf16[512]{0:T(512)(128)(2,1)S(1)}, bf16[512]{0:T(512)(128)(2,1)}, u32[]{:S(2)}) copy-start(bf16[512]{0:T(512)(128)(2,1)} %param.20) | copy-start | bytes 3076
  2.4 12.7 %all-to-all-start.2 = ((bf16[128,8,128]{2,0,1:T(8,128)(2,1)}), bf16[128,8,128]{2,0,1:T(8,128)(2,1)S(1)}, u32[]{:S(2)}, u32[]{:S(2)}) async-start(bf16[128,8,128]{2,0,1:T(8,128)(2,1)} %bitcast.11), calls=%async_computation.2 | async-start | bytes 524288 | tf_op jit(solution)/shard_map/all_to_all | solution.py:158
  12.1 37.5 %copy-start.8 = (f32[128,128]{1,0:T(8,128)}, f32[128,128]{1,0:T(8,128)S(1)}, u32[]{:S(2)}) copy-start(f32[128,128]{1,0:T(8,128)S(1)} %get-tuple-element.735) | copy-start | bytes 196612
  12.1 37.6 %copy-start.6 = (f32[128,128]{1,0:T(8,128)}, f32[128,128]{1,0:T(8,128)S(1)}, u32[]{:S(2)}) copy-start(f32[128,128]{1,0:T(8,128)S(1)} %get-tuple-element.734) | copy-start | bytes 196612
  15.8 9.5 %all-to-all-start.4 = ((bf16[128,8,128]{2,0,1:T(8,128)(2,1)}), bf16[128,8,128]{2,0,1:T(8,128)(2,1)S(1)}, u32[]{:S(2)}, u32[]{:S(2)}) async-start(bf16[128,8,128]{2,0,1:T(8,128)(2,1)} %bitcast.21), calls=%async_computation.4 | async-start | bytes 524288 | tf_op jit(solution)/shard_map/all_to_all | solution.py:159
  19.3 20.5 %copy-start.10 = (bf16[1,128,4096]{2,1,0:T(8,128)(2,1)S(1)}, bf16[1,128,4096]{2,1,0:T(8,128)(2,1)}, u32[]{:S(2)}) copy-start(bf16[1,128,4096]{2,1,0:T(8,128)(2,1)} %param.23) | copy-start | bytes 3145732
  25.3 15.8 %copy-start.13 = (bf16[128,8,128]{2,0,1:T(8,128)(2,1)}, bf16[128,8,128]{2,0,1:T(8,128)(2,1)S(1)}, u32[]{:S(2)}) copy-start(bf16[128,8,128]{2,0,1:T(8,128)(2,1)S(1)} %all-to-all-done.4) | copy-start | bytes 786436
  26.1 9.5 %all-to-all-start.5 = ((bf16[128,8,128]{2,0,1:T(8,128)(2,1)}), bf16[128,8,128]{2,0,1:T(8,128)(2,1)S(1)}, u32[]{:S(2)}, u32[]{:S(2)}) async-start(bf16[128,8,128]{2,0,1:T(8,128)(2,1)} %bitcast.26), calls=%async_computation.5 | async-start | bytes 524288 | tf_op jit(solution)/shard_map/all_to_all | solution.py:154
  36.4 9.5 %all-to-all-start.3 = ((bf16[128,8,128]{2,0,1:T(8,128)(2,1)}), bf16[128,8,128]{2,0,1:T(8,128)(2,1)S(1)}, u32[]{:S(2)}, u32[]{:S(2)}) async-start(bf16[128,8,128]{2,0,1:T(8,128)(2,1)} %bitcast.17), calls=%async_computation.3 | async-start | bytes 524288 | tf_op jit(solution)/shard_map/all_to_all | solution.py:153
  39.8 10.0 %copy-start.11 = (bf16[1,128,4096]{2,1,0:T(8,128)(2,1)S(1)}, bf16[1,128,4096]{2,1,0:T(8,128)(2,1)}, u32[]{:S(2)}) copy-start(bf16[1,128,4096]{2,1,0:T(8,128)(2,1)} %param.14) | copy-start | bytes 3145732
  45.9 3.8 %copy-start.17 = (bf16[128,8,128]{2,0,1:T(8,128)(2,1)}, bf16[128,8,128]{2,0,1:T(8,128)(2,1)S(1)}, u32[]{:S(2)}) copy-start(bf16[128,8,128]{2,0,1:T(8,128)(2,1)S(1)} %all-to-all-done.3) | copy-start | bytes 786436
  45.9 4.6 %copy-start.24 = (bf16[4096]{0:T(1024)(128)(2,1)S(1)}, bf16[4096]{0:T(1024)(128)(2,1)}, u32[]{:S(2)}) copy-start(bf16[4096]{0:T(1024)(128)(2,1)} %param.19) | copy-start | bytes 24580
  45.9 14.1 %all-to-all-start.1 = ((bf16[128,32,128]{0,2,1:T(8,128)(2,1)}), bf16[128,32,128]{0,2,1:T(8,128)(2,1)S(1)}, u32[]{:S(2)}, u32[]{:S(2)}) async-start(bf16[128,32,128]{0,2,1:T(8,128)(2,1)} %bitcast.6), calls=%async_computation.1 | async-start | bytes 2097152 | tf_op jit(solution)/shard_map/all_to_all | solution.py:155
  52.2 11.4 %copy-start.14 = (bf16[128,8,128]{2,0,1:T(8,128)(2,1)S(1)}, bf16[128,8,128]{2,0,1:T(8,128)(2,1)}, u32[]{:S(2)}) copy-start(bf16[128,8,128]{2,0,1:T(8,128)(2,1)} %copy-done.13) | copy-start | bytes 786436
  52.2 11.4 %copy-start.16 = (bf16[128,8,128]{2,0,1:T(8,128)(2,1)S(1)}, bf16[128,8,128]{2,0,1:T(8,128)(2,1)}, u32[]{:S(2)}) copy-start(bf16[128,8,128]{2,0,1:T(8,128)(2,1)} %copy-done.15) | copy-start | bytes 786436
  60.0 13.9 %all-to-all-start = ((bf16[128,32,128]{2,0,1:T(8,128)(2,1)}), bf16[128,32,128]{2,0,1:T(8,128)(2,1)S(1)}, u32[]{:S(2)}, u32[]{:S(2)}) async-start(bf16[128,32,128]{2,0,1:T(8,128)(2,1)} %copy.142), calls=%async_computation | async-start | bytes 2097152 | tf_op jit(solution)/shard_map/all_to_all | solution.py:152
  89.4 3.7 copy-start
  103.7 3.8 copy-start
  124.3 3.7 copy-start
  138.6 3.8 copy-start
  159.3 3.7 copy-start
  173.5 3.8 copy-start
  194.2 3.7 copy-start
  208.4 3.8 copy-start
  216.8 9.5 %all-to-all-start.8 = ((bf16[8,2,8192]{2,1,0:T(2,128)(2,1)}), bf16[8,2,8192]{2,1,0:T(2,128)(2,1)S(1)}, u32[]{:S(2)}, u32[]{:S(2)}) async-start(bf16[8,2,8192]{2,1,0:T(2,128)(2,1)} %reshape.436), calls=%async_computation.8 | async-start | bytes 524288 | tf_op jit(solution)/shard_map/all_to_all | solution.py:172
  226.3 10.0 %all-to-all-start.9 = ((bf16[8,2,8192]{2,1,0:T(2,128)(2,1)}), bf16[8,2,8192]{2,1,0:T(2,128)(2,1)S(1)}, u32[]{:S(2)}, u32[]{:S(2)}) async-start(bf16[8,2,8192]{2,1,0:T(2,128)(2,1)} %reshape.438), calls=%async_computation.9 | async-start | bytes 524288 | tf_op jit(solution)/shard_map/all_to_all | solution.py:175
  229.9 9.9 %copy-start.12 = (bf16[4,1024,1,128]{3,1,2,0:T(8,128)(2,1)S(1)}, bf16[4,1024,1,128]{3,1,2,0:T(8,128)(2,1)}, u32[]{:S(2)}) copy-start(bf16[4,1024,1,128]{3,1,2,0:T(8,128)(2,1)} %get-tuple-element.348) | copy-start | bytes 3145732
  236.2 15.3 %all-to-all-start.6 = ((bf16[1024,4,128]{2,1,0:T(4,128)(2,1)}), bf16[1024,4,128]{2,1,0:T(4,128)(2,1)S(1)}, u32[]{:S(2)}, u32[]{:S(2)}) async-start(bf16[1024,4,128]{2,1,0:T(4,128)(2,1)} %copy.153), calls=%async_computation.6 | async-start | bytes 2097152 | tf_op jit(solution)/shard_map/all_to_all | solution.py:168
  251.5 16.6 %all-to-all-start.7 = ((bf16[1024,4,128]{2,1,0:T(4,128)(2,1)}), bf16[1024,4,128]{2,1,0:T(4,128)(2,1)S(1)}, u32[]{:S(2)}, u32[]{:S(2)}) async-start(bf16[1024,4,128]{2,1,0:T(4,128)(2,1)} %bitcast.260), calls=%async_computation.7 | async-start | bytes 2097152 | tf_op jit(solution)/shard_map/all_to_all | solution.py:169
  255.4 5.0 %copy-start.9 = (f32[128,128]{1,0:T(8,128)S(1)}, f32[128,128]{1,0:T(8,128)}, u32[]{:S(2)}) copy-start(f32[128,128]{1,0:T(8,128)} %copy-done.8) | copy-start | bytes 196612
  (17 other events, 30.5 us)
where the time goes:
time: 379 us; the launch traced here: 376 us
  blocking collectives  90.5 us (24%)
  matrix products  79 us (21%)
  local copies, waits for them, and re-layouts  62 us (16%)
  waiting for transfers between devices  53.1 us (14%)
  starting transfers between devices  38.1 us (10%)
  other arithmetic  37.6 us (10%)
  loops' own time  14.1 us (4%)
    psum x1, blocking collectives, body(): lax.psum((jnp.sum(grad_query, axis=0).reshape(HQ * HD), jnp.sum(grad_key,...  90.5 us
    dot_general x8, matrix products, row_step(): jnp.einsum('hrk,kd->rhd', dscore, key_one, preferred_element_type=jnp.flo...  24.6 us
    dot_general x8, matrix products, row_step(): jnp.einsum('rhd,kd->hrk', cot_rows, value_one, preferred_element_type=jnp...  19.4 us
    dot_general x8, matrix products, row_step(): jnp.einsum('rhd,kd->hrk', query_rows, key_one, preferred_element_type=jnp...  18.6 us
    all_to_all x1, waiting for transfers between devices, body(): lax.all_to_all(outputs, 'seq', split_axis=0, concat_axis=1, tiled=True)  9.94 us
    another operation x1, loops' own time, attend(): lax.scan(head_step, (zeros_kv, zeros_kv), jnp.arange(heads // head_block,...  8.13 us
    unnamed x57, local copies, waits for them, and re-layouts  7.6 us
  transfers between devices with their start and end apart: 10, of which 10 were waited for; matrix products, arithmetic and copies ran while one was open for 7% of the time, Pallas kernels for 0%

commit v1 on v0

--- a/solution.py
+++ b/solution.py
@@ -181,12 +181,15 @@
     grad_query = rotary_back(dq_tokens.astype(jnp.float32), positions)
     grad_key = rotary_back(dk_tokens, positions)
     sums_query, sums_key, sums_value = lax.psum(
-        (
-            jnp.sum(grad_query, axis=0).reshape(HQ * HD),
-            jnp.sum(grad_key, axis=0).reshape(KV * HD),
-            jnp.sum(dv_tokens, axis=0).reshape(KV * HD),
+        lax.psum(
+            (
+                jnp.sum(grad_query, axis=0).reshape(HQ * HD),
+                jnp.sum(grad_key, axis=0).reshape(KV * HD),
+                jnp.sum(dv_tokens, axis=0).reshape(KV * HD),
+            ),
+            "seq",
         ),
-        ("dp", "seq"),
+        "dp",
     )
     return (
         out_tokens.reshape(1, tokens, HQ * HD),

time: 379 us -> 472 us (1.25)
  blocking collectives: 90.5 us -> 181 us
    psum x0 -> x1, blocking collectives: none -> 156 us  [body(): lax.psum(lax.psum((jnp.sum(grad_query, axis=0).reshape(HQ * HD), jnp.sum(...]
    psum x1, blocking collectives: 90.5 us -> 24.9 us  [body(): lax.psum((jnp.sum(grad_query, axis=0).reshape(HQ * HD), jnp.sum(grad_key,...]
  transfers between devices with their start and end apart: 10 -> 10, of which waited for: 10 -> 10; matrix products, arithmetic and copies ran while one was open for 7% -> 6% of each run, Pallas kernels for 0% -> 0%
where the time goes in v1:
time: 472 us; the launch traced here: 467 us
  blocking collectives  181 us (38%)
  matrix products  78.9 us (17%)
  local copies, waits for them, and re-layouts  62 us (13%)
  waiting for transfers between devices  53.2 us (11%)
  starting transfers between devices  38.1 us (8%)
  other arithmetic  37.6 us (8%)
  loops' own time  14.1 us (3%)
    psum x1, blocking collectives, body(): lax.psum(lax.psum((jnp.sum(grad_query, axis=0).reshape(HQ * HD), jnp.sum(...  156 us
    psum x1, blocking collectives, body(): lax.psum((jnp.sum(grad_query, axis=0).reshape(HQ * HD), jnp.sum(grad_key,...  24.9 us
    dot_general x8, matrix products, row_step(): jnp.einsum('hrk,kd->rhd', dscore, key_one, preferred_element_type=jnp.flo...  24.6 us
    dot_general x8, matrix products, row_step(): jnp.einsum('rhd,kd->hrk', cot_rows, value_one, preferred_element_type=jnp...  19.3 us
    dot_general x8, matrix products, row_step(): jnp.einsum('rhd,kd->hrk', query_rows, key_one, preferred_element_type=jnp...  18.5 us
    all_to_all x1, waiting for transfers between devices, body(): lax.all_to_all(outputs, 'seq', split_axis=0, concat_axis=1, tiled=True)  9.94 us
  transfers between devices with their start and end apart: 10, of which 10 were waited for; matrix products, arithmetic and copies ran while one was open for 6% of the time, Pallas kernels for 0%

profile of v1, /device:TPU:1, one launch (start us, length us, event | category | flops | bytes accessed | tf_op | source)
XLA Modules:
  0.0 466.6 jit_solution(10819471310725898682)
XLA Ops:
  2.4 6.5 %all-to-all-start.2 = ((bf16[128,8,128]{2,0,1:T(8,128)(2,1)}), bf16[128,8,128]{2,0,1:T(8,128)(2,1)S(1)}, u32[]{:S(2)}, u32[]{:S(2)}) async-start(bf16[128,8,128]{2,0,1:T(8,128)(2,1)} %bitcast.11), calls=%async_computation.2 | async-start | bytes 524288 | tf_op jit(solution)/shard_map/all_to_all | solution.py:158
  15.8 3.4 all-to-all-start.4
  19.3 6.0 %all-to-all-done.4 = bf16[128,8,128]{2,0,1:T(8,128)(2,1)S(1)} async-done(((bf16[128,8,128]{2,0,1:T(8,128)(2,1)}), bf16[128,8,128]{2,0,1:T(8,128)(2,1)S(1)}, u32[]{:S(2)}, u32[]{:S(2)}) %all-to-all-start.4) | async-done | bytes 262176 | tf_op jit(solution)/shard_map/all_to_all | solution.py:159
  26.1 3.4 all-to-all-start.5
  29.8 5.8 %all-to-all-done.5 = bf16[128,8,128]{2,0,1:T(8,128)(2,1)S(1)} async-done(((bf16[128,8,128]{2,0,1:T(8,128)(2,1)}), bf16[128,8,128]{2,0,1:T(8,128)(2,1)S(1)}, u32[]{:S(2)}, u32[]{:S(2)}) %all-to-all-start.5) | async-done | bytes 262176 | tf_op jit(solution)/shard_map/all_to_all | solution.py:154
  36.4 3.4 all-to-all-start.3
  41.2 4.7 %all-to-all-done.3 = bf16[128,8,128]{2,0,1:T(8,128)(2,1)S(1)} async-done(((bf16[128,8,128]{2,0,1:T(8,128)(2,1)}), bf16[128,8,128]{2,0,1:T(8,128)(2,1)S(1)}, u32[]{:S(2)}, u32[]{:S(2)}) %all-to-all-start.3) | async-done | bytes 262176 | tf_op jit(solution)/shard_map/all_to_all | solution.py:153
  45.9 3.7 all-to-all-start.1
  53.5 6.5 %all-to-all-done.1 = bf16[128,32,128]{0,2,1:T(8,128)(2,1)S(1)} async-done(((bf16[128,32,128]{0,2,1:T(8,128)(2,1)}), bf16[128,32,128]{0,2,1:T(8,128)(2,1)S(1)}, u32[]{:S(2)}, u32[]{:S(2)}) %all-to-all-start.1) | async-done | bytes 1048608 | tf_op jit(solution)/shard_map/all_to_all | solution.py:155
  60.0 3.6 all-to-all-start
  66.7 7.2 %all-to-all-done = bf16[128,32,128]{2,0,1:T(8,128)(2,1)S(1)} async-done(((bf16[128,32,128]{2,0,1:T(8,128)(2,1)}), bf16[128,32,128]{2,0,1:T(8,128)(2,1)S(1)}, u32[]{:S(2)}, u32[]{:S(2)}) %all-to-all-start) | async-done | bytes 1048608 | tf_op jit(solution)/shard_map/all_to_all | solution.py:152
  75.0 139.6 %while.59 = (s32[]{:T(128)}, f32[1024,1,128]{2,0,1:T(8,128)S(1)}, f32[1024,1,128]{2,0,1:T(8,128)S(1)}, bf16[4,1024,1,128]{3,1,2,0:T(8,128)(2,1)}, bf16[4,1024,1,...) while((s32[]{:T(128)}, f32[1024,1,128]{2,0,1:T(8,128)S(1)}, ...), condition=%wide.region_6.7_spmd.clone.clone, body=%wide.region_0.6_spmd.clone.clone.sunk | while | flops 1359287296 | bytes 49224388 | solution.py:116
  79.6 28.5 %while.60 = (s32[]{:T(128)}, f32[1024,128]{1,0:T(8,128)S(1)}, f32[1024,128]{1,0:T(8,128)S(1)}, bf16[2,512,1,128]{3,1,0,2:T(8,128)(2,1)}, bf16[2,512,1,128]{3,1,2...) while((s32[]{:T(128)}, f32[1024,128]{1,0:T(8,128)S(1)}, ...), condition=%wide.region_5.5_spmd.clone.clone, body=%wide.region_1.4_spmd.clone.clone.sunk | while | flops 1359025152 | bytes 41875732 | solution.py:104
  90.1 3.1 fusion.81
  104.3 3.1 fusion.81
  114.5 28.5 %while.60 = (s32[]{:T(128)}, f32[1024,128]{1,0:T(8,128)S(1)}, f32[1024,128]{1,0:T(8,128)S(1)}, bf16[2,512,1,128]{3,1,0,2:T(8,128)(2,1)}, bf16[2,512,1,128]{3,1,2...) while((s32[]{:T(128)}, f32[1024,128]{1,0:T(8,128)S(1)}, ...), condition=%wide.region_5.5_spmd.clone.clone, body=%wide.region_1.4_spmd.clone.clone.sunk | while | flops 1359025152 | bytes 41875732 | solution.py:104
  139.2 3.1 fusion.81
  149.3 28.5 %while.60 = (s32[]{:T(128)}, f32[1024,128]{1,0:T(8,128)S(1)}, f32[1024,128]{1,0:T(8,128)S(1)}, bf16[2,512,1,128]{3,1,0,2:T(8,128)(2,1)}, bf16[2,512,1,128]{3,1,2...) while((s32[]{:T(128)}, f32[1024,128]{1,0:T(8,128)S(1)}, ...), condition=%wide.region_5.5_spmd.clone.clone, body=%wide.region_1.4_spmd.clone.clone.sunk | while | flops 1359025152 | bytes 41875732 | solution.py:104
  174.1 3.1 fusion.81
  184.2 28.5 %while.60 = (s32[]{:T(128)}, f32[1024,128]{1,0:T(8,128)S(1)}, f32[1024,128]{1,0:T(8,128)S(1)}, bf16[2,512,1,128]{3,1,0,2:T(8,128)(2,1)}, bf16[2,512,1,128]{3,1,2...) while((s32[]{:T(128)}, f32[1024,128]{1,0:T(8,128)S(1)}, ...), condition=%wide.region_5.5_spmd.clone.clone, body=%wide.region_1.4_spmd.clone.clone.sunk | while | flops 1359025152 | bytes 41875732 | solution.py:104
  209.0 3.1 fusion.81
  216.7 3.4 all-to-all-start.8
  221.8 4.5 all-to-all-done.8
  226.2 3.6 all-to-all-start.9
  229.8 3.1 copy.153
  232.9 3.2 all-to-all-done.9
  236.2 3.6 all-to-all-start.6
  241.5 9.9 %all-to-all-done.6 = bf16[1024,4,128]{2,1,0:T(4,128)(2,1)S(1)} async-done(((bf16[1024,4,128]{2,1,0:T(4,128)(2,1)}), bf16[1024,4,128]{2,1,0:T(4,128)(2,1)S(1)}, u32[]{:S(2)}, u32[]{:S(2)}) %all-to-all-start.6) | async-done | bytes 1048608 | tf_op jit(solution)/shard_map/all_to_all | solution.py:168
  251.5 3.6 all-to-all-start.7
  273.0 3.2 copy.163
  285.9 24.9 %all-reduce.1 = (f32[4096]{0:T(1024)S(1)}, f32[512]{0:T(512)S(1)}, f32[512]{0:T(512)S(1)}) all-reduce(f32[4096]{0:T(1024)S(1)} %bitcast.274, f32[512]{0:T(512)S(1)} %bitcast.276, f32[512]{0:T(512)S(1)} %bitcast.277), channel_id=1, replica_groups=mesh['dp'=32,'seq'=8] {'seq'}, use_global_device_ids=true, to_apply=%region_10.11 | all-reduce | flops 5120 | bytes 40960 | tf_op jit(solution)/shard_map/psum | solution.py:184
  310.8 155.8 %all-reduce = (f32[4096]{0:T(1024)}, f32[512]{0:T(512)}, f32[512]{0:T(512)}) all-reduce(f32[4096]{0:T(1024)S(1)} %get-tuple-element.712, f32[512]{0:T(512)S(1)} %get-tuple-element.713, f32[512]{0:T(512)S(1)} %get-tuple-element.714), channel_id=1, replica_groups=mesh['dp'=32,'seq'=8] {'dp'}, use_global_device_ids=true, to_apply=%region_11.12 | all-reduce | flops 5120 | bytes 40960 | tf_op jit(solution)/shard_map/psum | solution.py:183
  (323 shorter events, 162.3 us)
Async XLA Ops:
  0.6 10.7 %copy-start.22 = (bf16[1,128,512]{2,1,0:T(8,128)(2,1)S(1)}, bf16[1,128,512]{2,1,0:T(8,128)(2,1)}, u32[]{:S(2)}) copy-start(bf16[1,128,512]{2,1,0:T(8,128)(2,1)} %param.15) | copy-start | bytes 393220
  0.6 10.9 %copy-start.23 = (bf16[1,128,512]{2,1,0:T(8,128)(2,1)S(1)}, bf16[1,128,512]{2,1,0:T(8,128)(2,1)}, u32[]{:S(2)}) copy-start(bf16[1,128,512]{2,1,0:T(8,128)(2,1)} %param.18) | copy-start | bytes 393220
  2.4 16.9 %copy-start.25 = (bf16[512]{0:T(512)(128)(2,1)S(1)}, bf16[512]{0:T(512)(128)(2,1)}, u32[]{:S(2)}) copy-start(bf16[512]{0:T(512)(128)(2,1)} %param.20) | copy-start | bytes 3076
  2.4 12.7 %all-to-all-start.2 = ((bf16[128,8,128]{2,0,1:T(8,128)(2,1)}), bf16[128,8,128]{2,0,1:T(8,128)(2,1)S(1)}, u32[]{:S(2)}, u32[]{:S(2)}) async-start(bf16[128,8,128]{2,0,1:T(8,128)(2,1)} %bitcast.11), calls=%async_computation.2 | async-start | bytes 524288 | tf_op jit(solution)/shard_map/all_to_all | solution.py:158
  12.1 37.5 %copy-start.8 = (f32[128,128]{1,0:T(8,128)}, f32[128,128]{1,0:T(8,128)S(1)}, u32[]{:S(2)}) copy-start(f32[128,128]{1,0:T(8,128)S(1)} %get-tuple-element.738) | copy-start | bytes 196612
  12.1 37.6 %copy-start.6 = (f32[128,128]{1,0:T(8,128)}, f32[128,128]{1,0:T(8,128)S(1)}, u32[]{:S(2)}) copy-start(f32[128,128]{1,0:T(8,128)S(1)} %get-tuple-element.737) | copy-start | bytes 196612
  15.8 9.5 %all-to-all-start.4 = ((bf16[128,8,128]{2,0,1:T(8,128)(2,1)}), bf16[128,8,128]{2,0,1:T(8,128)(2,1)S(1)}, u32[]{:S(2)}, u32[]{:S(2)}) async-start(bf16[128,8,128]{2,0,1:T(8,128)(2,1)} %bitcast.21), calls=%async_computation.4 | async-start | bytes 524288 | tf_op jit(solution)/shard_map/all_to_all | solution.py:159
  19.3 20.5 %copy-start.10 = (bf16[1,128,4096]{2,1,0:T(8,128)(2,1)S(1)}, bf16[1,128,4096]{2,1,0:T(8,128)(2,1)}, u32[]{:S(2)}) copy-start(bf16[1,128,4096]{2,1,0:T(8,128)(2,1)} %param.23) | copy-start | bytes 3145732
  25.3 15.8 %copy-start.13 = (bf16[128,8,128]{2,0,1:T(8,128)(2,1)}, bf16[128,8,128]{2,0,1:T(8,128)(2,1)S(1)}, u32[]{:S(2)}) copy-start(bf16[128,8,128]{2,0,1:T(8,128)(2,1)S(1)} %all-to-all-done.4) | copy-start | bytes 786436
  26.1 9.5 %all-to-all-start.5 = ((bf16[128,8,128]{2,0,1:T(8,128)(2,1)}), bf16[128,8,128]{2,0,1:T(8,128)(2,1)S(1)}, u32[]{:S(2)}, u32[]{:S(2)}) async-start(bf16[128,8,128]{2,0,1:T(8,128)(2,1)} %bitcast.26), calls=%async_computation.5 | async-start | bytes 524288 | tf_op jit(solution)/shard_map/all_to_all | solution.py:154
  36.4 9.5 %all-to-all-start.3 = ((bf16[128,8,128]{2,0,1:T(8,128)(2,1)}), bf16[128,8,128]{2,0,1:T(8,128)(2,1)S(1)}, u32[]{:S(2)}, u32[]{:S(2)}) async-start(bf16[128,8,128]{2,0,1:T(8,128)(2,1)} %bitcast.17), calls=%async_computation.3 | async-start | bytes 524288 | tf_op jit(solution)/shard_map/all_to_all | solution.py:153
  39.8 10.0 %copy-start.11 = (bf16[1,128,4096]{2,1,0:T(8,128)(2,1)S(1)}, bf16[1,128,4096]{2,1,0:T(8,128)(2,1)}, u32[]{:S(2)}) copy-start(bf16[1,128,4096]{2,1,0:T(8,128)(2,1)} %param.14) | copy-start | bytes 3145732
  45.9 3.8 copy-start.17
  45.9 4.6 copy-start.24
  45.9 14.1 %all-to-all-start.1 = ((bf16[128,32,128]{0,2,1:T(8,128)(2,1)}), bf16[128,32,128]{0,2,1:T(8,128)(2,1)S(1)}, u32[]{:S(2)}, u32[]{:S(2)}) async-start(bf16[128,32,128]{0,2,1:T(8,128)(2,1)} %bitcast.6), calls=%async_computation.1 | async-start | bytes 2097152 | tf_op jit(solution)/shard_map/all_to_all | solution.py:155
  52.2 11.4 %copy-start.14 = (bf16[128,8,128]{2,0,1:T(8,128)(2,1)S(1)}, bf16[128,8,128]{2,0,1:T(8,128)(2,1)}, u32[]{:S(2)}) copy-start(bf16[128,8,128]{2,0,1:T(8,128)(2,1)} %copy-done.13) | copy-start | bytes 786436
  52.2 11.4 %copy-start.16 = (bf16[128,8,128]{2,0,1:T(8,128)(2,1)S(1)}, bf16[128,8,128]{2,0,1:T(8,128)(2,1)}, u32[]{:S(2)}) copy-start(bf16[128,8,128]{2,0,1:T(8,128)(2,1)} %copy-done.15) | copy-start | bytes 786436
  60.0 13.9 %all-to-all-start = ((bf16[128,32,128]{2,0,1:T(8,128)(2,1)}), bf16[128,32,128]{2,0,1:T(8,128)(2,1)S(1)}, u32[]{:S(2)}, u32[]{:S(2)}) async-start(bf16[128,32,128]{2,0,1:T(8,128)(2,1)} %copy.142), calls=%async_computation | async-start | bytes 2097152 | tf_op jit(solution)/shard_map/all_to_all | solution.py:152
  89.4 3.7 copy-start
  103.7 3.7 copy-start
  124.3 3.7 copy-start
  138.6 3.7 copy-start
  159.2 3.7 copy-start
  173.5 3.7 copy-start
  194.1 3.7 copy-start
  208.4 3.7 copy-start
  216.7 9.5 %all-to-all-start.8 = ((bf16[8,2,8192]{2,1,0:T(2,128)(2,1)}), bf16[8,2,8192]{2,1,0:T(2,128)(2,1)S(1)}, u32[]{:S(2)}, u32[]{:S(2)}) async-start(bf16[8,2,8192]{2,1,0:T(2,128)(2,1)} %reshape.436), calls=%async_computation.8 | async-start | bytes 524288 | tf_op jit(solution)/shard_map/all_to_all | solution.py:172
  226.2 10.0 %all-to-all-start.9 = ((bf16[8,2,8192]{2,1,0:T(2,128)(2,1)}), bf16[8,2,8192]{2,1,0:T(2,128)(2,1)S(1)}, u32[]{:S(2)}, u32[]{:S(2)}) async-start(bf16[8,2,8192]{2,1,0:T(2,128)(2,1)} %reshape.438), calls=%async_computation.9 | async-start | bytes 524288 | tf_op jit(solution)/shard_map/all_to_all | solution.py:175
  229.8 9.9 %copy-start.12 = (bf16[4,1024,1,128]{3,1,2,0:T(8,128)(2,1)S(1)}, bf16[4,1024,1,128]{3,1,2,0:T(8,128)(2,1)}, u32[]{:S(2)}) copy-start(bf16[4,1024,1,128]{3,1,2,0:T(8,128)(2,1)} %get-tuple-element.348) | copy-start | bytes 3145732
  236.2 15.3 %all-to-all-start.6 = ((bf16[1024,4,128]{2,1,0:T(4,128)(2,1)}), bf16[1024,4,128]{2,1,0:T(4,128)(2,1)S(1)}, u32[]{:S(2)}, u32[]{:S(2)}) async-start(bf16[1024,4,128]{2,1,0:T(4,128)(2,1)} %copy.153), calls=%async_computation.6 | async-start | bytes 2097152 | tf_op jit(solution)/shard_map/all_to_all | solution.py:168
  251.5 16.6 %all-to-all-start.7 = ((bf16[1024,4,128]{2,1,0:T(4,128)(2,1)}), bf16[1024,4,128]{2,1,0:T(4,128)(2,1)S(1)}, u32[]{:S(2)}, u32[]{:S(2)}) async-start(bf16[1024,4,128]{2,1,0:T(4,128)(2,1)} %bitcast.260), calls=%async_computation.7 | async-start | bytes 2097152 | tf_op jit(solution)/shard_map/all_to_all | solution.py:169
  255.4 5.0 %copy-start.9 = (f32[128,128]{1,0:T(8,128)S(1)}, f32[128,128]{1,0:T(8,128)}, u32[]{:S(2)}) copy-start(f32[128,128]{1,0:T(8,128)} %copy-done.8) | copy-start | bytes 196612
  (17 other events, 30.5 us)
